TPU v7x, 32 devices: a whole 2x2x4 slice. The times are simulated.
32 devices in a mesh: section: 4 (over y, x), frame: 4 (over z), row: 2 (over core).
Axes of the slice: x: 2, y: 2, z: 4, core: 2. Of those that a mesh axis runs over, the one named last changes fastest.
Arguments:
- x_saved: bfloat16 [4, 8, 16, 64, 128], P('section', 'frame', 'row'), may hold values from -6 to 6
- cotangent: bfloat16 [8, 16, 64, 128], P('frame', 'row'), may hold values from -6 to 6
- w_spatial: bfloat16 [4, 3, 3, 128, 128], P('section'), may hold values from -0.1875 to 0.1875
- w_temporal: bfloat16 [4, 3, 128, 128], P('section'), may hold values from -0.3125 to 0.3125
Outputs:
- grad_inputs: bfloat16 [4, 8, 16, 64, 128], P('section', 'frame', 'row')
- grad_spatial: float32 [4, 3, 3, 128, 128], P('section')
- grad_temporal: float32 [4, 3, 128, 128], P('section')
All inputs are finite; a program needn't handle non-finite values.
Results may differ from a plain program's by a relative error of at most 0.014.
Values may be sent and summed in bfloat16 or wider, within the bound.
No kernel may reach another device: no remote copies, remote signals or barrier semaphores. Data moves between devices by JAX's collectives and lax.ppermute only.
A program may use at most 64 MiB of HBM per device.

v0:
```python
import jax
import jax.numpy as jnp
from jax import lax
from jax.sharding import PartitionSpec as P


def padded_2(cells, sides, width):
    for axis, dim in sides:
        count = lax.axis_size(axis)
        ends = count - 1
        head = lax.slice_in_dim(cells, 0, width, axis=dim)
        tail = lax.slice_in_dim(cells, cells.shape[dim] - width, cells.shape[dim], axis=dim)
        cells = jnp.concatenate(
            [
                lax.ppermute(tail, axis, [(i, (i + 1) % count) for i in range(ends)]),
                cells,
                lax.ppermute(head, axis, [((i + 1) % count, i) for i in range(ends)]),
            ],
            axis=dim,
        )
    return cells


def from_behind(block, axis, distance):
    devices = range(lax.axis_size(axis))
    route = [(i - distance, i) for i in devices if i - distance in devices]
    return lax.ppermute(block, axis, route)


def slope_of(pre_act):
    sigma = jax.nn.sigmoid(pre_act)
    return sigma * (1.0 + pre_act * (1.0 - sigma))


def inner_sum(first_arg, second_arg):
    return lax.dot_general(
        first_arg, second_arg, (((0,), (0,)), ((), ())), preferred_element_type=jnp.float32
    )


def pad_cols(values):
    return jnp.pad(values, ((0, 0), (0, 0), (1, 1), (0, 0)))


def frame_shift(values, offset, max_reach):
    widths = [(max_reach, max_reach)] + [(0, 0)] * (values.ndim - 1)
    padded = jnp.pad(values, widths)
    return lax.dynamic_slice_in_dim(padded, max_reach + offset, values.shape[0], 0)


def apply_taps(padded, taps, row_count, col_count, transpose):
    channels = padded.shape[-1]
    running = jnp.zeros((padded.shape[0] * row_count * col_count, taps.shape[-1]), jnp.float32)
    for i in range(3):
        for j in range(3):
            window = padded[:, i : i + row_count, j : j + col_count, :].reshape(-1, channels)
            if transpose:
                running = running + jnp.dot(
                    window, taps[2 - i, 2 - j].T, preferred_element_type=jnp.float32
                )
            else:
                running = running + jnp.dot(window, taps[i, j], preferred_element_type=jnp.float32)
    return running.reshape(padded.shape[0], row_count, col_count, taps.shape[-1])


def to_blocks(values, frame_parts):
    frame_count, row_count, col_count, channels = values.shape
    return values.reshape(frame_count, frame_parts, row_count * col_count // frame_parts, channels)


def temporal_back(segment, taps_time, dilation, max_reach):
    channels = segment.shape[-1]
    running = jnp.zeros((segment.size // channels, channels), jnp.float32)
    for k in range(3):
        shifted = frame_shift(segment, (1 - k) * dilation, max_reach).reshape(-1, channels)
        running = running + jnp.dot(shifted, taps_time[k].T, preferred_element_type=jnp.float32)
    return running.astype(jnp.bfloat16).reshape(segment.shape)


def spatial_back(back_tiles, pre_slope, taps_space, local_shape):
    back_act = lax.all_to_all(back_tiles, "frame", split_axis=0, concat_axis=1, tiled=True).reshape(
        local_shape
    )
    grad_pre = (back_act.astype(jnp.float32) * pre_slope).astype(jnp.bfloat16)
    rims = padded_2(grad_pre, (("row", 1),), 1)
    branch = apply_taps(pad_cols(rims), taps_space, local_shape[1], local_shape[2], True).astype(
        jnp.bfloat16
    )
    return (grad_pre, branch)


def pass_back(outgoing):
    return from_behind(outgoing, "section", -1)


def section_run(x_saved, cotangent, w_spatial, w_temporal):
    block_input = x_saved[0]
    taps_space = w_spatial[0]
    taps_time = w_temporal[0]
    local_shape = block_input.shape
    row_count = local_shape[1]
    col_count = local_shape[2]
    channels = local_shape[3]
    frame_parts = lax.axis_size("frame")
    section_count = lax.axis_size("section")
    section_index = lax.axis_index("section")
    dilation = jnp.left_shift(jnp.int32(1), section_index)
    max_reach = 2 ** (section_count - 1)
    extended = pad_cols(padded_2(block_input, (("row", 1),), 1))
    pre_act = apply_taps(extended, taps_space, row_count, col_count, False)
    pre_slope = slope_of(pre_act)
    active = jax.nn.silu(pre_act).astype(jnp.bfloat16)
    active_tiles = lax.all_to_all(
        to_blocks(active, frame_parts), "frame", split_axis=1, concat_axis=0, tiled=True
    )
    kept_pre = jnp.zeros(local_shape, jnp.bfloat16)
    kept_tiles = jnp.zeros_like(active_tiles)
    incoming = cotangent
    own_grad = jnp.zeros(local_shape, jnp.bfloat16)
    for position in range(section_count):
        with_segment = lax.all_to_all(
            to_blocks(incoming, frame_parts), "frame", split_axis=1, concat_axis=0, tiled=True
        )
        back_tiles = temporal_back(with_segment, taps_time, dilation, max_reach)
        grad_pre, branch = spatial_back(back_tiles, pre_slope, taps_space, local_shape)
        outgoing = (
            incoming.astype(jnp.float32) + lax.optimization_barrier(branch).astype(jnp.float32)
        ).astype(jnp.bfloat16)
        is_owner = section_index == section_count - 1 - position
        own_grad = jnp.where(is_owner, outgoing, own_grad)
        kept_pre = jnp.where(is_owner, grad_pre, kept_pre)
        kept_tiles = jnp.where(is_owner, with_segment, kept_tiles)
        if position + 1 < section_count:
            incoming = pass_back(outgoing)
    flat_pre = kept_pre.reshape(-1, channels)
    grads_space = jnp.stack(
        [
            jnp.stack(
                [
                    inner_sum(
                        extended[:, i : i + row_count, j : j + col_count, :].reshape(-1, channels),
                        flat_pre,
                    )
                    for j in range(3)
                ]
            )
            for i in range(3)
        ]
    )
    flat_tiles = kept_tiles.reshape(-1, channels)
    grads_time = jnp.stack(
        [
            inner_sum(
                frame_shift(active_tiles, (k - 1) * dilation, max_reach).reshape(-1, channels),
                flat_tiles,
            )
            for k in range(3)
        ]
    )
    grads_space, grads_time = lax.psum((grads_space, grads_time), ("frame", "row"))
    return (own_grad[None], grads_space[None], grads_time[None])


def local(x_saved, cotangent, w_spatial, w_temporal):
    return section_run(x_saved, cotangent, w_spatial, w_temporal)


def solution(mesh):
    return jax.shard_map(
        local,
        mesh=mesh,
        in_specs=(
            P("section", "frame", "row", None, None),
            P("frame", "row", None, None),
            P("section", None, None, None, None),
            P("section", None, None, None),
        ),
        out_specs=(
            P("section", "frame", "row", None, None),
            P("section", None, None, None, None),
            P("section", None, None, None),
        ),
        check_vma=False,
    )
```

profile of v0, /device:TPU:0, one launch (start us, length us, event | category | flops | bytes accessed | tf_op | source)
XLA Modules:
  0.0 260.1 jit_solution(2147495361420427421)
XLA Ops:
  7.2 0.8 fusion.101
  8.0 2.3 collective-permute-start
  10.3 1.3 collective-permute-start.1
  11.6 1.7 copy.56
  13.3 5.8 %all-to-all-start = ((bf16[2,4,128,128]{3,2,0,1:T(8,128)(2,1)}), bf16[2,4,128,128]{3,2,0,1:T(8,128)(2,1)S(1)}, u32[]{:S(2)}, u32[]{:S(2)}) async-start(bf16[2,4,128,128]{3,2,0,1:T(8,128)(2,1)} %copy.56), calls=%async_computation | async-start | bytes 524288 | tf_op jit(solution)/shard_map/all_to_all | solution.py:121
  19.5 0.7 copy-done
  20.5 0.7 pad_maximum_fusion.8
  22.3 7.0 %all-to-all-done = bf16[2,4,128,128]{3,2,0,1:T(8,128)(2,1)S(1)} async-done(((bf16[2,4,128,128]{3,2,0,1:T(8,128)(2,1)}), bf16[2,4,128,128]{3,2,0,1:T(8,128)(2,1)S(1)}, u32[]{:S(2)}, u32[]{:S(2)}) %all-to-all-start) | async-done | bytes 262176 | tf_op jit(solution)/shard_map/all_to_all | solution.py:121
  29.4 0.8 copy-done.8
  30.6 0.9 fusion.9
  31.6 3.4 %all-to-all-start.1 = ((bf16[8,1,128,128]{3,2,1,0:T(8,128)(2,1)}), bf16[8,1,128,128]{3,2,1,0:T(8,128)(2,1)S(1)}, u32[]{:S(2)}, u32[]{:S(2)}) async-start(bf16[8,1,128,128]{3,2,1,0:T(8,128)(2,1)} %bitcast.12), calls=%async_computation.1 | async-start | bytes 524288 | tf_op jit(solution)/shard_map/all_to_all | solution.py:81
  35.2 1.0 convolution_add_fusion.35
  36.2 8.1 %all-to-all-done.1 = bf16[8,1,128,128]{3,2,1,0:T(8,128)(2,1)S(1)} async-done(((bf16[8,1,128,128]{3,2,1,0:T(8,128)(2,1)}), bf16[8,1,128,128]{3,2,1,0:T(8,128)(2,1)S(1)}, u32[]{:S(2)}, u32[]{:S(2)}) %all-to-all-start.1) | async-done | bytes 262176 | tf_op jit(solution)/shard_map/all_to_all | solution.py:81
  44.3 0.7 copy-done.2
  45.0 1.0 copy-done.18
  46.1 0.4 fusion.17
  46.7 1.3 collective-permute-start.2
  48.0 1.3 collective-permute-start.3
  49.3 1.8 collective-permute-done.3
  53.7 0.7 copy-done.9
  54.5 1.3 collective-permute-start.4
  55.8 9.0 %collective-permute-done.4 = bf16[2,8,64,128]{3,2,1,0:T(8,128)(2,1)S(1)} collective-permute-done((bf16[2,8,64,128]{3,2,1,0:T(8,128)(2,1)S(1)}, bf16[2,8,64,128]{3,2,1,0:T(8,128)(2,1)S(1)}, u32[]{:S(2)}, u32[]{:S(2)}) %collective-permute-start.4) | collective-permute-done | bytes 262176 | tf_op jit(solution)/shard_map/ppermute | solution.py:27
  64.8 11.1 %all_to_all.126 = bf16[2,4,128,128]{3,2,0,1:T(8,128)(2,1)S(1)} all-to-all(bf16[2,4,128,128]{3,2,0,1:T(8,128)(2,1)S(1)} %copy.61), channel_id=1, replica_groups=mesh['section'=4,'frame'=4,'row'=2] {'frame'}, dimensions={1} | all-to-all | bytes 524288 | tf_op jit(solution)/shard_map/all_to_all | solution.py:121
  76.7 10.9 %all_to_all.127 = bf16[8,1,128,128]{3,2,1,0:T(8,128)(2,1)S(1)} all-to-all(bf16[8,1,128,128]{3,2,1,0:T(8,128)(2,1)S(1)} %bitcast.560), channel_id=1, replica_groups=mesh['section'=4,'frame'=4,'row'=2] {'frame'}, dimensions={0} | all-to-all | bytes 524288 | tf_op jit(solution)/shard_map/all_to_all | solution.py:81
  87.6 0.7 copy-done.4
  88.6 1.3 collective-permute-start.5
  89.9 1.3 collective-permute-start.6
  91.4 1.6 collective-permute-done.6
  95.6 1.3 collective-permute-start.7
  96.9 9.6 %collective-permute-done.7 = bf16[2,8,64,128]{3,2,1,0:T(8,128)(2,1)S(1)} collective-permute-done((bf16[2,8,64,128]{3,2,1,0:T(8,128)(2,1)S(1)}, bf16[2,8,64,128]{3,2,1,0:T(8,128)(2,1)S(1)}, u32[]{:S(2)}, u32[]{:S(2)}) %collective-permute-start.7) | collective-permute-done | bytes 262176 | tf_op jit(solution)/shard_map/ppermute | solution.py:27
  106.5 11.3 %all_to_all.128 = bf16[2,4,128,128]{3,2,0,1:T(8,128)(2,1)S(1)} all-to-all(bf16[2,4,128,128]{3,2,0,1:T(8,128)(2,1)S(1)} %copy.66), channel_id=1, replica_groups=mesh['section'=4,'frame'=4,'row'=2] {'frame'}, dimensions={1} | all-to-all | bytes 524288 | tf_op jit(solution)/shard_map/all_to_all | solution.py:121
  118.7 10.9 %all_to_all.129 = bf16[8,1,128,128]{3,2,1,0:T(8,128)(2,1)S(1)} all-to-all(bf16[8,1,128,128]{3,2,1,0:T(8,128)(2,1)S(1)} %bitcast.561), channel_id=1, replica_groups=mesh['section'=4,'frame'=4,'row'=2] {'frame'}, dimensions={0} | all-to-all | bytes 524288 | tf_op jit(solution)/shard_map/all_to_all | solution.py:81
  129.7 0.7 copy-done.6
  130.6 1.3 collective-permute-start.8
  131.9 1.3 collective-permute-start.9
  133.4 1.6 collective-permute-done.9
  137.7 0.7 copy-done.14
  138.4 1.3 collective-permute-start.10
  139.6 9.6 %collective-permute-done.10 = bf16[2,8,64,128]{3,2,1,0:T(8,128)(2,1)S(1)} collective-permute-done((bf16[2,8,64,128]{3,2,1,0:T(8,128)(2,1)S(1)}, bf16[2,8,64,128]{3,2,1,0:T(8,128)(2,1)S(1)}, u32[]{:S(2)}, u32[]{:S(2)}) %collective-permute-start.10) | collective-permute-done | bytes 262176 | tf_op jit(solution)/shard_map/ppermute | solution.py:27
  149.2 0.8 copy.71
  150.0 3.4 %all-to-all-start.6 = ((bf16[2,4,128,128]{3,2,0,1:T(8,128)(2,1)}), bf16[2,4,128,128]{3,2,0,1:T(8,128)(2,1)S(1)}, u32[]{:S(2)}, u32[]{:S(2)}) async-start(bf16[2,4,128,128]{3,2,0,1:T(8,128)(2,1)} %copy.71), calls=%async_computation.6 | async-start | bytes 524288 | tf_op jit(solution)/shard_map/all_to_all | solution.py:121
  153.5 1.0 copy.81
  154.5 1.9 multiply_convert_fusion
  156.4 6.1 %all-to-all-done.6 = bf16[2,4,128,128]{3,2,0,1:T(8,128)(2,1)S(1)} async-done(((bf16[2,4,128,128]{3,2,0,1:T(8,128)(2,1)}), bf16[2,4,128,128]{3,2,0,1:T(8,128)(2,1)S(1)}, u32[]{:S(2)}, u32[]{:S(2)}) %all-to-all-start.6) | async-done | bytes 262176 | tf_op jit(solution)/shard_map/all_to_all | solution.py:121
  162.4 4.1 %all-to-all-start.8 = ((bf16[2,4,128,128]{2,3,0,1:T(8,128)(2,1)}), bf16[2,4,128,128]{2,3,0,1:T(8,128)(2,1)}, u32[]{:S(2)}, u32[]{:S(2)}) async-start(bf16[2,4,128,128]{2,3,0,1:T(8,128)(2,1)} %multiply_convert_fusion), calls=%async_computation.8 | async-start | bytes 524288 | tf_op jit(solution)/shard_map/all_to_all | solution.py:113
  167.1 0.9 fusion.12
  168.1 5.4 %all-to-all-done.8 = bf16[2,4,128,128]{2,3,0,1:T(8,128)(2,1)} async-done(((bf16[2,4,128,128]{2,3,0,1:T(8,128)(2,1)}), bf16[2,4,128,128]{2,3,0,1:T(8,128)(2,1)}, u32[]{:S(2)}, u32[]{:S(2)}) %all-to-all-start.8) | async-done | bytes 262176 | tf_op jit(solution)/shard_map/all_to_all | solution.py:113
  173.5 3.4 %all-to-all-start.7 = ((bf16[8,1,128,128]{3,2,1,0:T(8,128)(2,1)}), bf16[8,1,128,128]{3,2,1,0:T(8,128)(2,1)S(1)}, u32[]{:S(2)}, u32[]{:S(2)}) async-start(bf16[8,1,128,128]{3,2,1,0:T(8,128)(2,1)} %bitcast.550), calls=%async_computation.7 | async-start | bytes 524288 | tf_op jit(solution)/shard_map/all_to_all | solution.py:81
  177.2 1.2 convolution_bitcast_fusion.4
  178.4 1.2 convolution_bitcast_fusion.3
  179.5 1.2 convolution_bitcast_fusion.2
  180.7 0.7 maximum_bitcast_fusion.4
  181.4 2.3 all-to-all-done.7
  186.0 0.7 copy-done.3
  186.9 0.4 fusion.31
  187.6 1.3 collective-permute-start.11
  188.9 1.3 collective-permute-start.12
  190.6 0.7 copy-done.22
  191.6 0.9 maximum_bitcast_fusion
  195.1 0.7 copy-done.11
  196.0 0.8 fusion.30
  196.8 53.8 %all-reduce.13.cloned.1.call-done = (f32[1,3,3,128,128]{4,3,2,1,0:T(8,128)}, f32[1,3,128,128]{3,2,1,0:T(8,128)}) async-done(((f32[1,3,3,128,128]{4,3,2,1,0:T(8,128)}, f32[1,3,128,128]{3,2,1,0:T(8,128)}), (f32[1,3,3,128,128]{4,3,2,1,0:T(8,128)}, f32[1,3,128,128]{3,2,1,0:T(8,128)})) %all-reduce.13.cloned.1.call-update) | async-done | bytes 786448 | tf_op jit(solution)/shard_map/psum | solution.py:160
  250.6 2.0 copy.98
  252.6 0.7 copy.99
  (156 shorter events, 20.2 us)
Async XLA Ops:
  8.0 11.2 %collective-permute-start = (bf16[2,1,64,128]{3,2,1,0:T(8,128)(2,1)S(1)}, bf16[2,1,64,128]{3,2,1,0:T(8,128)(2,1)S(1)}, u32[]{:S(2)}, u32[]{:S(2)}) collective-permute-start(bf16[2,1,64,128]{3,2,1,0:T(8,128)(2,1)S(1)} %get-tuple-element.61), channel_id=1, source_target_pairs={{0,1},{2,3},{4,5},{6,7},{8,9},{10,11},{12,13},{14,15},{16,17},{18,... | collective-permute-start | bytes 98312 | tf_op jit(solution)/shard_map/ppermute | solution.py:15
  10.3 8.8 %collective-permute-start.1 = (bf16[2,1,64,128]{3,2,1,0:T(8,128)(2,1)S(1)}, bf16[2,1,64,128]{3,2,1,0:T(8,128)(2,1)S(1)}, u32[]{:S(2)}, u32[]{:S(2)}) collective-permute-start(bf16[2,1,64,128]{3,2,1,0:T(8,128)(2,1)S(1)} %get-tuple-element.62), channel_id=1, source_target_pairs={{1,0},{3,2},{5,4},{7,6},{9,8},{11,10},{13,12},{15,14},{17,16},{19,... | collective-permute-start | bytes 98312 | tf_op jit(solution)/shard_map/ppermute | solution.py:17
  13.3 5.8 %copy-start.1 = (bf16[1,2,8,64,128]{4,3,2,1,0:T(8,128)(2,1)S(1)}, bf16[1,2,8,64,128]{4,3,2,1,0:T(8,128)(2,1)}, u32[]{:S(2)}) copy-start(bf16[1,2,8,64,128]{4,3,2,1,0:T(8,128)(2,1)} %param.4) | copy-start | bytes 786436
  13.3 16.0 %all-to-all-start = ((bf16[2,4,128,128]{3,2,0,1:T(8,128)(2,1)}), bf16[2,4,128,128]{3,2,0,1:T(8,128)(2,1)S(1)}, u32[]{:S(2)}, u32[]{:S(2)}) async-start(bf16[2,4,128,128]{3,2,0,1:T(8,128)(2,1)} %copy.56), calls=%async_computation | async-start | bytes 524288 | tf_op jit(solution)/shard_map/all_to_all | solution.py:121
  19.1 1.3 copy-start.21
  19.1 1.3 copy-start.23
  19.3 1.0 copy-start
  29.3 0.9 copy-start.8
  31.6 12.7 %all-to-all-start.1 = ((bf16[8,1,128,128]{3,2,1,0:T(8,128)(2,1)}), bf16[8,1,128,128]{3,2,1,0:T(8,128)(2,1)S(1)}, u32[]{:S(2)}, u32[]{:S(2)}) async-start(bf16[8,1,128,128]{3,2,1,0:T(8,128)(2,1)} %bitcast.12), calls=%async_computation.1 | async-start | bytes 524288 | tf_op jit(solution)/shard_map/all_to_all | solution.py:81
  44.3 0.7 copy-start.2
  45.0 1.0 copy-start.18
  45.0 1.1 copy-start.19
  46.7 2.6 %collective-permute-start.2 = (bf16[2,1,64,128]{3,2,1,0:T(8,128)(2,1)S(1)}, bf16[2,1,64,128]{3,2,1,0:T(8,128)(2,1)S(1)}, u32[]{:S(2)}, u32[]{:S(2)}) collective-permute-start(bf16[2,1,64,128]{3,2,1,0:T(8,128)(2,1)S(1)} %get-tuple-element.57), channel_id=1, source_target_pairs={{0,1},{2,3},{4,5},{6,7},{8,9},{10,11},{12,13},{14,15},{16,17},{18,... | collective-permute-start | bytes 98312 | tf_op jit(solution)/shard_map/ppermute | solution.py:15
  48.0 3.1 %collective-permute-start.3 = (bf16[2,1,64,128]{3,2,1,0:T(8,128)(2,1)S(1)}, bf16[2,1,64,128]{3,2,1,0:T(8,128)(2,1)S(1)}, u32[]{:S(2)}, u32[]{:S(2)}) collective-permute-start(bf16[2,1,64,128]{3,2,1,0:T(8,128)(2,1)S(1)} %get-tuple-element.58), channel_id=1, source_target_pairs={{1,0},{3,2},{5,4},{7,6},{9,8},{11,10},{13,12},{15,14},{17,16},{19,... | collective-permute-start | bytes 98312 | tf_op jit(solution)/shard_map/ppermute | solution.py:17
  53.4 1.0 copy-start.9
  54.5 10.3 %copy-start.10 = (bf16[2,8,64,128]{3,2,1,0:T(8,128)(2,1)}, bf16[2,8,64,128]{3,2,1,0:T(8,128)(2,1)S(1)}, u32[]{:S(2)}) copy-start(bf16[2,8,64,128]{3,2,1,0:T(8,128)(2,1)S(1)} %add_convert_fusion.3) | copy-start | bytes 786436
  54.5 10.3 %collective-permute-start.4 = (bf16[2,8,64,128]{3,2,1,0:T(8,128)(2,1)S(1)}, bf16[2,8,64,128]{3,2,1,0:T(8,128)(2,1)S(1)}, u32[]{:S(2)}, u32[]{:S(2)}) collective-permute-start(bf16[2,8,64,128]{3,2,1,0:T(8,128)(2,1)S(1)} %add_convert_fusion.3), channel_id=1, source_target_pairs={{8,0},{16,8},{24,16},{9,1},{17,9},{25,17},{10,2},{18,10},{26,18},{... | collective-permute-start | bytes 786440 | tf_op jit(solution)/shard_map/ppermute | solution.py:27
  87.6 0.7 copy-start.4
  88.6 2.8 %collective-permute-start.5 = (bf16[2,1,64,128]{3,2,1,0:T(8,128)(2,1)S(1)}, bf16[2,1,64,128]{3,2,1,0:T(8,128)(2,1)S(1)}, u32[]{:S(2)}, u32[]{:S(2)}) collective-permute-start(bf16[2,1,64,128]{3,2,1,0:T(8,128)(2,1)S(1)} %get-tuple-element.51), channel_id=1, source_target_pairs={{0,1},{2,3},{4,5},{6,7},{8,9},{10,11},{12,13},{14,15},{16,17},{18,... | collective-permute-start | bytes 98312 | tf_op jit(solution)/shard_map/ppermute | solution.py:15
  89.9 3.1 %collective-permute-start.6 = (bf16[2,1,64,128]{3,2,1,0:T(8,128)(2,1)S(1)}, bf16[2,1,64,128]{3,2,1,0:T(8,128)(2,1)S(1)}, u32[]{:S(2)}, u32[]{:S(2)}) collective-permute-start(bf16[2,1,64,128]{3,2,1,0:T(8,128)(2,1)S(1)} %get-tuple-element.52), channel_id=1, source_target_pairs={{1,0},{3,2},{5,4},{7,6},{9,8},{11,10},{13,12},{15,14},{17,16},{19,... | collective-permute-start | bytes 98312 | tf_op jit(solution)/shard_map/ppermute | solution.py:17
  95.6 10.9 %copy-start.12 = (bf16[2,8,64,128]{3,2,1,0:T(8,128)(2,1)}, bf16[2,8,64,128]{3,2,1,0:T(8,128)(2,1)S(1)}, u32[]{:S(2)}) copy-start(bf16[2,8,64,128]{3,2,1,0:T(8,128)(2,1)S(1)} %add_convert_fusion.2) | copy-start | bytes 786436
  95.6 10.9 %collective-permute-start.7 = (bf16[2,8,64,128]{3,2,1,0:T(8,128)(2,1)S(1)}, bf16[2,8,64,128]{3,2,1,0:T(8,128)(2,1)S(1)}, u32[]{:S(2)}, u32[]{:S(2)}) collective-permute-start(bf16[2,8,64,128]{3,2,1,0:T(8,128)(2,1)S(1)} %add_convert_fusion.2), channel_id=1, source_target_pairs={{8,0},{16,8},{24,16},{9,1},{17,9},{25,17},{10,2},{18,10},{26,18},{... | collective-permute-start | bytes 786440 | tf_op jit(solution)/shard_map/ppermute | solution.py:27
  129.6 0.7 copy-start.6
  130.6 2.8 %collective-permute-start.8 = (bf16[2,1,64,128]{3,2,1,0:T(8,128)(2,1)S(1)}, bf16[2,1,64,128]{3,2,1,0:T(8,128)(2,1)S(1)}, u32[]{:S(2)}, u32[]{:S(2)}) collective-permute-start(bf16[2,1,64,128]{3,2,1,0:T(8,128)(2,1)S(1)} %get-tuple-element.45), channel_id=1, source_target_pairs={{0,1},{2,3},{4,5},{6,7},{8,9},{10,11},{12,13},{14,15},{16,17},{18,... | collective-permute-start | bytes 98312 | tf_op jit(solution)/shard_map/ppermute | solution.py:15
  131.9 3.1 %collective-permute-start.9 = (bf16[2,1,64,128]{3,2,1,0:T(8,128)(2,1)S(1)}, bf16[2,1,64,128]{3,2,1,0:T(8,128)(2,1)S(1)}, u32[]{:S(2)}, u32[]{:S(2)}) collective-permute-start(bf16[2,1,64,128]{3,2,1,0:T(8,128)(2,1)S(1)} %get-tuple-element.46), channel_id=1, source_target_pairs={{1,0},{3,2},{5,4},{7,6},{9,8},{11,10},{13,12},{15,14},{17,16},{19,... | collective-permute-start | bytes 98312 | tf_op jit(solution)/shard_map/ppermute | solution.py:17
  137.7 0.7 copy-start.14
  138.4 10.9 %collective-permute-start.10 = (bf16[2,8,64,128]{3,2,1,0:T(8,128)(2,1)S(1)}, bf16[2,8,64,128]{3,2,1,0:T(8,128)(2,1)S(1)}, u32[]{:S(2)}, u32[]{:S(2)}) collective-permute-start(bf16[2,8,64,128]{3,2,1,0:T(8,128)(2,1)S(1)} %add_convert_fusion.1), channel_id=1, source_target_pairs={{8,0},{16,8},{24,16},{9,1},{17,9},{25,17},{10,2},{18,10},{26,18},{... | collective-permute-start | bytes 786440 | tf_op jit(solution)/shard_map/ppermute | solution.py:27
  149.2 0.8 copy-start.16
  150.0 12.4 %all-to-all-start.6 = ((bf16[2,4,128,128]{3,2,0,1:T(8,128)(2,1)}), bf16[2,4,128,128]{3,2,0,1:T(8,128)(2,1)S(1)}, u32[]{:S(2)}, u32[]{:S(2)}) async-start(bf16[2,4,128,128]{3,2,0,1:T(8,128)(2,1)} %copy.71), calls=%async_computation.6 | async-start | bytes 524288 | tf_op jit(solution)/shard_map/all_to_all | solution.py:121
  162.4 11.1 %all-to-all-start.8 = ((bf16[2,4,128,128]{2,3,0,1:T(8,128)(2,1)}), bf16[2,4,128,128]{2,3,0,1:T(8,128)(2,1)}, u32[]{:S(2)}, u32[]{:S(2)}) async-start(bf16[2,4,128,128]{2,3,0,1:T(8,128)(2,1)} %multiply_convert_fusion), calls=%async_computation.8 | async-start | bytes 524288 | tf_op jit(solution)/shard_map/all_to_all | solution.py:113
  173.5 10.2 %all-to-all-start.7 = ((bf16[8,1,128,128]{3,2,1,0:T(8,128)(2,1)}), bf16[8,1,128,128]{3,2,1,0:T(8,128)(2,1)S(1)}, u32[]{:S(2)}, u32[]{:S(2)}) async-start(bf16[8,1,128,128]{3,2,1,0:T(8,128)(2,1)} %bitcast.550), calls=%async_computation.7 | async-start | bytes 524288 | tf_op jit(solution)/shard_map/all_to_all | solution.py:81
  176.9 73.7 %all-reduce.13.cloned.1.call-start = ((), (), s32[]{:S(2)}) async-start(), calls=%async_computation.9 | async-start | bytes 1572864 | tf_op jit(solution)/shard_map/psum | solution.py:160
  185.8 1.0 copy-start.3
  185.8 1.0 copy-start.5
  185.8 1.1 copy-start.7
  187.6 2.6 %copy-start.24 = (bf16[2,1,64,128]{3,2,1,0:T(8,128)(2,1)S(1)}, bf16[2,1,64,128]{3,2,1,0:T(8,128)(2,1)}, u32[]{:S(2)}) copy-start(bf16[2,1,64,128]{3,2,1,0:T(8,128)(2,1)} %copy-done.23) | copy-start | bytes 98308
  187.6 4.9 %collective-permute-start.11 = (bf16[2,1,64,128]{3,2,1,0:T(8,128)(2,1)S(1)}, bf16[2,1,64,128]{3,2,1,0:T(8,128)(2,1)S(1)}, u32[]{:S(2)}, u32[]{:S(2)}) collective-permute-start(bf16[2,1,64,128]{3,2,1,0:T(8,128)(2,1)S(1)} %get-tuple-element.39), channel_id=1, source_target_pairs={{0,1},{2,3},{4,5},{6,7},{8,9},{10,11},{12,13},{14,15},{16,17},{18,... | collective-permute-start | bytes 98312 | tf_op jit(solution)/shard_map/ppermute | solution.py:15
  188.9 3.6 %collective-permute-start.12 = (bf16[2,1,64,128]{3,2,1,0:T(8,128)(2,1)S(1)}, bf16[2,1,64,128]{3,2,1,0:T(8,128)(2,1)S(1)}, u32[]{:S(2)}, u32[]{:S(2)}) collective-permute-start(bf16[2,1,64,128]{3,2,1,0:T(8,128)(2,1)S(1)} %get-tuple-element.40), channel_id=1, source_target_pairs={{1,0},{3,2},{5,4},{7,6},{9,8},{11,10},{13,12},{15,14},{17,16},{19,... | collective-permute-start | bytes 98312 | tf_op jit(solution)/shard_map/ppermute | solution.py:17
  190.5 0.8 copy-start.22
  194.8 1.0 copy-start.11
  194.8 1.0 copy-start.13
  194.9 1.1 copy-start.15
  194.9 1.2 copy-start.17
  250.6 2.0 copy-start.20
Sparse Core Ops, SparseCore 0:
  192.6 57.9 all-reduce.12
where the time goes:
time: 262 us; the launch traced here: 260 us
  waiting for transfers between devices  116 us (44%)
  blocking collectives  44.2 us (17%)
  starting transfers between devices  38.2 us (15%)
  matrix products  21.1 us (8%)
  local copies, waits for them, and re-layouts  17.5 us (7%)
  between operations  15.1 us (6%)
  other arithmetic  8.21 us (3%)
    psum x1, waiting for transfers between devices, section_run(): lax.psum((grads_space, grads_time), ('frame', 'row'))  53.8 us
    ppermute x3, waiting for transfers between devices, from_behind(): return lax.ppermute(block, axis, route)  28.2 us
    all_to_all x2, blocking collectives, section_run(): lax.all_to_all(to_blocks(incoming, frame_parts), 'frame', split_axis=1, c...  22.4 us
    all_to_all x2, blocking collectives, spatial_back(): lax.all_to_all(back_tiles, 'frame', split_axis=0, concat_axis=1, tiled=True)  21.8 us
    all_to_all x2, waiting for transfers between devices, section_run(): lax.all_to_all(to_blocks(incoming, frame_parts), 'frame', split_axis=1, c...  13.1 us
    unnamed x52, local copies, waits for them, and re-layouts  11.2 us
    all_to_all x2, waiting for transfers between devices, spatial_back(): lax.all_to_all(back_tiles, 'frame', split_axis=0, concat_axis=1, tiled=True)  10.4 us
    all_to_all x2, starting transfers between devices, section_run(): lax.all_to_all(to_blocks(incoming, frame_parts), 'frame', split_axis=1, c...  9.24 us
  transfers between devices with their start and end apart: 19, of which 12 were waited for; matrix products, arithmetic and copies ran while one was open for 7% of the time, Pallas kernels for 0%

commit v1 on v0

--- a/solution.py
+++ b/solution.py
@@ -2,6 +2,17 @@
 import jax.numpy as jnp
 from jax import lax
 from jax.sharding import PartitionSpec as P
+
+
+def split_up(shard, dim, size):
+    before, after = (shard.shape[:dim], shard.shape[dim + 1 :])
+    return jnp.moveaxis(shard.reshape(*before, size, -1, *after), dim, 0)
+
+
+def joined_along(blocks, dim):
+    shape = list(blocks.shape[1:])
+    shape[dim] *= blocks.shape[0]
+    return jnp.moveaxis(blocks, 0, dim).reshape(shape)
 
 
 def padded_2(cells, sides, width):
@@ -118,9 +129,15 @@
     incoming = cotangent
     own_grad = jnp.zeros(local_shape, jnp.bfloat16)
     for position in range(section_count):
-        with_segment = lax.all_to_all(
-            to_blocks(incoming, frame_parts), "frame", split_axis=1, concat_axis=0, tiled=True
-        )
+        x = to_blocks(incoming, frame_parts)
+        size, position_2 = (lax.axis_size("frame"), lax.axis_index("frame"))
+        blocks = split_up(x, 1, size)
+        gathered = [blocks[position_2]]
+        for step in range(1, size):
+            sent = blocks[position_2 ^ step]
+            gathered.append(lax.ppermute(sent, "frame", [(i_2, i_2 ^ step) for i_2 in range(size)]))
+        blocks = jnp.stack(gathered)[position_2 ^ jnp.arange(size)]
+        with_segment = joined_along(blocks, 0)
         back_tiles = temporal_back(with_segment, taps_time, dilation, max_reach)
         grad_pre, branch = spatial_back(back_tiles, pre_slope, taps_space, local_shape)
         outgoing = (

time: 262 us -> 249 us (0.950)
  blocking collectives: 44.2 us -> 20.9 us
  starting transfers between devices: 38.2 us -> 47.8 us
  waiting for transfers between devices: 116 us -> 112 us
    all_to_all x2 -> x0, blocking collectives: 22.4 us -> none  [section_run(): lax.all_to_all(to_blocks(incoming, frame_parts), 'frame', split_axis=1, c...]
    ppermute x0 -> x12, starting transfers between devices: none -> 18.4 us  [section_run(): lax.ppermute(sent, 'frame', [(i_2, i_2 ^ step) for i_2 in range(size)])]
    all_to_all x2 -> x0, waiting for transfers between devices: 13.1 us -> none  [section_run(): lax.all_to_all(to_blocks(incoming, frame_parts), 'frame', split_axis=1, c...]
    ppermute x0 -> x12, waiting for transfers between devices: none -> 12.3 us  [section_run(): lax.ppermute(sent, 'frame', [(i_2, i_2 ^ step) for i_2 in range(size)])]
    all_to_all x2 -> x0, starting transfers between devices: 9.24 us -> none  [section_run(): lax.all_to_all(to_blocks(incoming, frame_parts), 'frame', split_axis=1, c...]
    dynamic_slice x0 -> x4, local copies, waits for them, and re-layouts: none -> 2.67 us  [section_run(): gathered = [blocks[position_2]]]
    unnamed x52 -> x48, local copies, waits for them, and re-layouts: 11.2 us -> 11 us
  transfers between devices with their start and end apart: 19 -> 29, of which waited for: 12 -> 16; matrix products, arithmetic and copies ran while one was open for 7% -> 8% of each run, Pallas kernels for 0% -> 0%
where the time goes in v1:
time: 249 us; the launch traced here: 247 us
  waiting for transfers between devices  112 us (45%)
  starting transfers between devices  47.8 us (19%)
  matrix products  21.8 us (9%)
  blocking collectives  20.9 us (8%)
  local copies, waits for them, and re-layouts  19.2 us (8%)
  between operations  15.3 us (6%)
  other arithmetic  9.99 us (4%)
    psum x1, waiting for transfers between devices, section_run(): lax.psum((grads_space, grads_time), ('frame', 'row'))  53.1 us
    ppermute x3, waiting for transfers between devices, from_behind(): return lax.ppermute(block, axis, route)  28 us
    all_to_all x2, blocking collectives, spatial_back(): lax.all_to_all(back_tiles, 'frame', split_axis=0, concat_axis=1, tiled=True)  20.9 us
    ppermute x12, starting transfers between devices, section_run(): lax.ppermute(sent, 'frame', [(i_2, i_2 ^ step) for i_2 in range(size)])  18.4 us
    ppermute x12, waiting for transfers between devices, section_run(): lax.ppermute(sent, 'frame', [(i_2, i_2 ^ step) for i_2 in range(size)])  12.3 us
    unnamed x48, local copies, waits for them, and re-layouts  11 us
    all_to_all x2, waiting for transfers between devices, spatial_back(): lax.all_to_all(back_tiles, 'frame', split_axis=0, concat_axis=1, tiled=True)  9.51 us
    dot_general x36, matrix products, apply_taps(): jnp.dot(window, taps[2 - i, 2 - j].T, preferred_element_type=jnp.float32)  8.1 us
  transfers between devices with their start and end apart: 29, of which 16 were waited for; matrix products, arithmetic and copies ran while one was open for 8% of the time, Pallas kernels for 0%

profile of v1, /device:TPU:0, one launch (start us, length us, event | category | flops | bytes accessed | tf_op | source)
XLA Modules:
  0.0 247.1 jit_solution(9126088394080294758)
XLA Ops:
  7.2 0.8 fusion.101
  8.0 2.3 collective-permute-start.3
  10.3 1.3 collective-permute-start.4
  11.6 1.0 dynamic-slice_bitcast_fusion.15
  12.7 2.5 collective-permute-start
  15.1 2.6 %collective-permute-start.1 = (bf16[2,1,128,128]{3,2,0,1:T(8,128)(2,1)S(1)}, bf16[2,1,128,128]{3,2,0,1:T(8,128)(2,1)S(1)}, u32[]{:S(2)}, u32[]{:S(2)}) collective-permute-start(bf16[2,1,128,128]{3,2,0,1:T(8,128)(2,1)S(1)} %get-tuple-element.79), channel_id=1, source_target_pairs={{0,4},{2,6},{4,0},{6,2},{1,5},{3,7},{5,1},{7,3},{8,12},{10,14},{12... | collective-permute-start | bytes 196616 | tf_op jit(solution)/shard_map/ppermute | solution.py:138
  20.3 2.1 collective-permute-done.1
  22.4 1.9 collective-permute-done.2
  24.3 0.9 maximum_bitcast_fusion.1
  25.9 0.7 copy-done.8
  27.1 0.9 fusion.9
  28.1 3.8 %all-to-all-start = ((bf16[8,1,128,128]{3,2,1,0:T(8,128)(2,1)}), bf16[8,1,128,128]{3,2,1,0:T(8,128)(2,1)S(1)}, u32[]{:S(2)}, u32[]{:S(2)}) async-start(bf16[8,1,128,128]{3,2,1,0:T(8,128)(2,1)} %bitcast.18), calls=%async_computation | async-start | bytes 524288 | tf_op jit(solution)/shard_map/all_to_all | solution.py:92
  31.8 1.0 fusion.77
  32.8 1.0 convolution_add_fusion.35
  33.9 7.0 %all-to-all-done = bf16[8,1,128,128]{3,2,1,0:T(8,128)(2,1)S(1)} async-done(((bf16[8,1,128,128]{3,2,1,0:T(8,128)(2,1)}), bf16[8,1,128,128]{3,2,1,0:T(8,128)(2,1)S(1)}, u32[]{:S(2)}, u32[]{:S(2)}) %all-to-all-start) | async-done | bytes 262176 | tf_op jit(solution)/shard_map/all_to_all | solution.py:92
  41.7 1.0 copy-done.15
  43.4 1.3 collective-permute-start.5
  44.7 1.3 collective-permute-start.6
  46.0 1.8 collective-permute-done.6
  51.1 1.3 collective-permute-start.7
  52.4 9.0 %collective-permute-done.7 = bf16[2,8,64,128]{3,2,1,0:T(8,128)(2,1)S(1)} collective-permute-done((bf16[2,8,64,128]{3,2,1,0:T(8,128)(2,1)S(1)}, bf16[2,8,64,128]{3,2,1,0:T(8,128)(2,1)S(1)}, u32[]{:S(2)}, u32[]{:S(2)}) %collective-permute-start.7) | collective-permute-done | bytes 262176 | tf_op jit(solution)/shard_map/ppermute | solution.py:38
  61.7 1.8 collective-permute-start.9
  63.5 2.4 collective-permute-start.10
  65.9 2.7 %collective-permute-done.9 = bf16[2,1,128,128]{3,2,0,1:T(8,128)(2,1)S(1)} collective-permute-done((bf16[2,1,128,128]{3,2,0,1:T(8,128)(2,1)S(1)}, bf16[2,1,128,128]{3,2,0,1:T(8,128)(2,1)S(1)}, u32[]{:S(2)}, u32[]{:S(2)}) %collective-permute-start.9) | collective-permute-done | bytes 65568 | tf_op jit(solution)/shard_map/ppermute | solution.py:138
  68.6 1.0 collective-permute-done.10
  71.2 10.5 %all_to_all.54 = bf16[8,1,128,128]{3,2,1,0:T(8,128)(2,1)S(1)} all-to-all(bf16[8,1,128,128]{3,2,1,0:T(8,128)(2,1)S(1)} %bitcast.581), channel_id=1, replica_groups=mesh['section'=4,'frame'=4,'row'=2] {'frame'}, dimensions={0} | all-to-all | bytes 524288 | tf_op jit(solution)/shard_map/all_to_all | solution.py:92
  82.6 1.3 collective-permute-start.11
  83.9 1.3 collective-permute-start.12
  85.5 1.6 collective-permute-done.12
  89.7 1.3 collective-permute-start.13
  91.0 9.6 %collective-permute-done.13 = bf16[2,8,64,128]{3,2,1,0:T(8,128)(2,1)S(1)} collective-permute-done((bf16[2,8,64,128]{3,2,1,0:T(8,128)(2,1)S(1)}, bf16[2,8,64,128]{3,2,1,0:T(8,128)(2,1)S(1)}, u32[]{:S(2)}, u32[]{:S(2)}) %collective-permute-start.13) | collective-permute-done | bytes 262176 | tf_op jit(solution)/shard_map/ppermute | solution.py:38
  100.6 1.2 collective-permute-start.14
  101.8 1.1 collective-permute-start.15
  102.8 2.2 collective-permute-start.16
  105.4 4.1 %collective-permute-done.15 = bf16[2,1,128,128]{3,2,0,1:T(8,128)(2,1)S(1)} collective-permute-done((bf16[2,1,128,128]{3,2,0,1:T(8,128)(2,1)S(1)}, bf16[2,1,128,128]{3,2,0,1:T(8,128)(2,1)S(1)}, u32[]{:S(2)}, u32[]{:S(2)}) %collective-permute-start.15) | collective-permute-done | bytes 65568 | tf_op jit(solution)/shard_map/ppermute | solution.py:138
  111.1 10.4 %all_to_all.55 = bf16[8,1,128,128]{3,2,1,0:T(8,128)(2,1)S(1)} all-to-all(bf16[8,1,128,128]{3,2,1,0:T(8,128)(2,1)S(1)} %bitcast.582), channel_id=1, replica_groups=mesh['section'=4,'frame'=4,'row'=2] {'frame'}, dimensions={0} | all-to-all | bytes 524288 | tf_op jit(solution)/shard_map/all_to_all | solution.py:92
  122.5 1.3 collective-permute-start.17
  123.8 1.3 collective-permute-start.18
  125.3 1.6 collective-permute-done.18
  129.4 0.8 add_convert_fusion.1
  130.2 1.3 collective-permute-start.19
  131.7 9.5 %collective-permute-done.19 = bf16[2,8,64,128]{3,2,1,0:T(8,128)(2,1)} collective-permute-done((bf16[2,8,64,128]{3,2,1,0:T(8,128)(2,1)}, bf16[2,8,64,128]{3,2,1,0:T(8,128)(2,1)}, u32[]{:S(2)}, u32[]{:S(2)}) %collective-permute-start.19) | collective-permute-done | bytes 262176 | tf_op jit(solution)/shard_map/ppermute | solution.py:38
  141.2 1.6 dynamic-slice_bitcast_fusion.3
  142.8 1.0 collective-permute-start.20
  143.9 1.1 collective-permute-start.21
  145.0 2.2 collective-permute-start.22
  147.2 0.8 multiply_convert_fusion
  148.1 4.4 %all-to-all-start.4 = ((bf16[2,4,128,128]{2,3,0,1:T(8,128)(2,1)}), bf16[2,4,128,128]{2,3,0,1:T(8,128)(2,1)}, u32[]{:S(2)}, u32[]{:S(2)}) async-start(bf16[2,4,128,128]{2,3,0,1:T(8,128)(2,1)} %multiply_convert_fusion), calls=%async_computation.4 | async-start | bytes 524288 | tf_op jit(solution)/shard_map/all_to_all | solution.py:124
  152.5 0.9 maximum_bitcast_fusion.4
  154.2 0.7 copy-done.9
  155.4 0.9 fusion.12
  156.4 4.1 %all-to-all-done.4 = bf16[2,4,128,128]{2,3,0,1:T(8,128)(2,1)} async-done(((bf16[2,4,128,128]{2,3,0,1:T(8,128)(2,1)}), bf16[2,4,128,128]{2,3,0,1:T(8,128)(2,1)}, u32[]{:S(2)}, u32[]{:S(2)}) %all-to-all-start.4) | async-done | bytes 262176 | tf_op jit(solution)/shard_map/all_to_all | solution.py:124
  160.5 3.4 %all-to-all-start.3 = ((bf16[8,1,128,128]{3,2,1,0:T(8,128)(2,1)}), bf16[8,1,128,128]{3,2,1,0:T(8,128)(2,1)S(1)}, u32[]{:S(2)}, u32[]{:S(2)}) async-start(bf16[8,1,128,128]{3,2,1,0:T(8,128)(2,1)} %bitcast.571), calls=%async_computation.3 | async-start | bytes 524288 | tf_op jit(solution)/shard_map/all_to_all | solution.py:92
  163.9 1.2 convolution_bitcast_fusion.4
  165.1 1.2 convolution_bitcast_fusion.3
  166.3 1.2 convolution_bitcast_fusion.2
  168.2 2.5 %all-to-all-done.3 = bf16[8,1,128,128]{3,2,1,0:T(8,128)(2,1)S(1)} async-done(((bf16[8,1,128,128]{3,2,1,0:T(8,128)(2,1)}), bf16[8,1,128,128]{3,2,1,0:T(8,128)(2,1)S(1)}, u32[]{:S(2)}, u32[]{:S(2)}) %all-to-all-start.3) | async-done | bytes 262176 | tf_op jit(solution)/shard_map/all_to_all | solution.py:92
  174.6 1.3 collective-permute-start.23
  175.9 1.3 collective-permute-start.24
  177.5 0.7 copy-done.20
  178.5 0.9 maximum_bitcast_fusion
  182.8 1.8 fusion.30
  184.5 53.1 %all-reduce.13.cloned.1.call-done = (f32[1,3,3,128,128]{4,3,2,1,0:T(8,128)}, f32[1,3,128,128]{3,2,1,0:T(8,128)}) async-done(((f32[1,3,3,128,128]{4,3,2,1,0:T(8,128)}, f32[1,3,128,128]{3,2,1,0:T(8,128)}), (f32[1,3,3,128,128]{4,3,2,1,0:T(8,128)}, f32[1,3,128,128]{3,2,1,0:T(8,128)})) %all-reduce.13.cloned.1.call-update) | async-done | bytes 786448 | tf_op jit(solution)/shard_map/psum | solution.py:177
  237.7 2.0 copy.78
  (180 shorter events, 29.7 us)
Async XLA Ops:
  8.0 9.8 %collective-permute-start.3 = (bf16[2,1,64,128]{3,2,1,0:T(8,128)(2,1)S(1)}, bf16[2,1,64,128]{3,2,1,0:T(8,128)(2,1)S(1)}, u32[]{:S(2)}, u32[]{:S(2)}) collective-permute-start(bf16[2,1,64,128]{3,2,1,0:T(8,128)(2,1)S(1)} %get-tuple-element.73), channel_id=1, source_target_pairs={{0,1},{2,3},{4,5},{6,7},{8,9},{10,11},{12,13},{14,15},{16,17},{18,... | collective-permute-start | bytes 98312 | tf_op jit(solution)/shard_map/ppermute | solution.py:26
  10.3 7.5 %collective-permute-start.4 = (bf16[2,1,64,128]{3,2,1,0:T(8,128)(2,1)S(1)}, bf16[2,1,64,128]{3,2,1,0:T(8,128)(2,1)S(1)}, u32[]{:S(2)}, u32[]{:S(2)}) collective-permute-start(bf16[2,1,64,128]{3,2,1,0:T(8,128)(2,1)S(1)} %get-tuple-element.74), channel_id=1, source_target_pairs={{1,0},{3,2},{5,4},{7,6},{9,8},{11,10},{13,12},{15,14},{17,16},{19,... | collective-permute-start | bytes 98312 | tf_op jit(solution)/shard_map/ppermute | solution.py:28
  11.6 6.2 %copy-start.1 = (bf16[1,2,8,64,128]{4,3,2,1,0:T(8,128)(2,1)S(1)}, bf16[1,2,8,64,128]{4,3,2,1,0:T(8,128)(2,1)}, u32[]{:S(2)}) copy-start(bf16[1,2,8,64,128]{4,3,2,1,0:T(8,128)(2,1)} %param.4) | copy-start | bytes 786436
  12.7 7.6 %collective-permute-start = (bf16[2,1,128,128]{3,2,0,1:T(8,128)(2,1)S(1)}, bf16[2,1,128,128]{3,2,0,1:T(8,128)(2,1)S(1)}, u32[]{:S(2)}, u32[]{:S(2)}) collective-permute-start(bf16[2,1,128,128]{3,2,0,1:T(8,128)(2,1)S(1)} %get-tuple-element.80), channel_id=1, source_target_pairs={{0,2},{2,0},{4,6},{6,4},{1,3},{3,1},{5,7},{7,5},{8,10},{10,8},{12,... | collective-permute-start | bytes 196616 | tf_op jit(solution)/shard_map/ppermute | solution.py:138
  15.1 7.3 %collective-permute-start.1 = (bf16[2,1,128,128]{3,2,0,1:T(8,128)(2,1)S(1)}, bf16[2,1,128,128]{3,2,0,1:T(8,128)(2,1)S(1)}, u32[]{:S(2)}, u32[]{:S(2)}) collective-permute-start(bf16[2,1,128,128]{3,2,0,1:T(8,128)(2,1)S(1)} %get-tuple-element.79), channel_id=1, source_target_pairs={{0,4},{2,6},{4,0},{6,2},{1,5},{3,7},{5,1},{7,3},{8,12},{10,14},{12... | collective-permute-start | bytes 196616 | tf_op jit(solution)/shard_map/ppermute | solution.py:138
  17.7 6.6 %collective-permute-start.2 = (bf16[2,1,128,128]{3,2,0,1:T(8,128)(2,1)S(1)}, bf16[2,1,128,128]{3,2,0,1:T(8,128)(2,1)}, u32[]{:S(2)}, u32[]{:S(2)}) collective-permute-start(bf16[2,1,128,128]{3,2,0,1:T(8,128)(2,1)S(1)} %get-tuple-element.78), channel_id=1, source_target_pairs={{0,6},{2,4},{4,2},{6,0},{1,7},{3,5},{5,3},{7,1},{8,14},{10,12},{12... | collective-permute-start | bytes 196616 | tf_op jit(solution)/shard_map/ppermute | solution.py:138
  17.8 1.3 copy-start.19
  17.8 1.3 copy-start.21
  17.9 1.0 copy-start
  25.8 0.9 copy-start.8
  28.1 12.9 %all-to-all-start = ((bf16[8,1,128,128]{3,2,1,0:T(8,128)(2,1)}), bf16[8,1,128,128]{3,2,1,0:T(8,128)(2,1)S(1)}, u32[]{:S(2)}, u32[]{:S(2)}) async-start(bf16[8,1,128,128]{3,2,1,0:T(8,128)(2,1)} %bitcast.18), calls=%async_computation | async-start | bytes 524288 | tf_op jit(solution)/shard_map/all_to_all | solution.py:92
  40.9 0.7 copy-start.2
  41.6 1.0 copy-start.15
  41.6 1.2 copy-start.16
  43.4 2.6 %collective-permute-start.5 = (bf16[2,1,64,128]{3,2,1,0:T(8,128)(2,1)S(1)}, bf16[2,1,64,128]{3,2,1,0:T(8,128)(2,1)S(1)}, u32[]{:S(2)}, u32[]{:S(2)}) collective-permute-start(bf16[2,1,64,128]{3,2,1,0:T(8,128)(2,1)S(1)} %get-tuple-element.69), channel_id=1, source_target_pairs={{0,1},{2,3},{4,5},{6,7},{8,9},{10,11},{12,13},{14,15},{16,17},{18,... | collective-permute-start | bytes 98312 | tf_op jit(solution)/shard_map/ppermute | solution.py:26
  44.7 3.1 %collective-permute-start.6 = (bf16[2,1,64,128]{3,2,1,0:T(8,128)(2,1)S(1)}, bf16[2,1,64,128]{3,2,1,0:T(8,128)(2,1)S(1)}, u32[]{:S(2)}, u32[]{:S(2)}) collective-permute-start(bf16[2,1,64,128]{3,2,1,0:T(8,128)(2,1)S(1)} %get-tuple-element.70), channel_id=1, source_target_pairs={{1,0},{3,2},{5,4},{7,6},{9,8},{11,10},{13,12},{15,14},{17,16},{19,... | collective-permute-start | bytes 98312 | tf_op jit(solution)/shard_map/ppermute | solution.py:28
  50.1 1.0 copy-start.10
  51.1 10.3 %copy-start.11 = (bf16[2,8,64,128]{3,2,1,0:T(8,128)(2,1)}, bf16[2,8,64,128]{3,2,1,0:T(8,128)(2,1)S(1)}, u32[]{:S(2)}) copy-start(bf16[2,8,64,128]{3,2,1,0:T(8,128)(2,1)S(1)} %add_convert_fusion.3) | copy-start | bytes 786436
  51.1 10.3 %collective-permute-start.7 = (bf16[2,8,64,128]{3,2,1,0:T(8,128)(2,1)S(1)}, bf16[2,8,64,128]{3,2,1,0:T(8,128)(2,1)S(1)}, u32[]{:S(2)}, u32[]{:S(2)}) collective-permute-start(bf16[2,8,64,128]{3,2,1,0:T(8,128)(2,1)S(1)} %add_convert_fusion.3), channel_id=1, source_target_pairs={{8,0},{16,8},{24,16},{9,1},{17,9},{25,17},{10,2},{18,10},{26,18},{... | collective-permute-start | bytes 786440 | tf_op jit(solution)/shard_map/ppermute | solution.py:38
  61.4 4.5 %collective-permute-start.8 = (bf16[2,1,128,128]{3,2,0,1:T(8,128)(2,1)S(1)}, bf16[2,1,128,128]{3,2,0,1:T(8,128)(2,1)S(1)}, u32[]{:S(2)}, u32[]{:S(2)}) collective-permute-start(bf16[2,1,128,128]{3,2,0,1:T(8,128)(2,1)S(1)} %get-tuple-element.66), channel_id=1, source_target_pairs={{0,2},{2,0},{4,6},{6,4},{1,3},{3,1},{5,7},{7,5},{8,10},{10,8},{12,... | collective-permute-start | bytes 196616 | tf_op jit(solution)/shard_map/ppermute | solution.py:138
  61.7 7.0 %collective-permute-start.9 = (bf16[2,1,128,128]{3,2,0,1:T(8,128)(2,1)S(1)}, bf16[2,1,128,128]{3,2,0,1:T(8,128)(2,1)S(1)}, u32[]{:S(2)}, u32[]{:S(2)}) collective-permute-start(bf16[2,1,128,128]{3,2,0,1:T(8,128)(2,1)S(1)} %get-tuple-element.65), channel_id=1, source_target_pairs={{0,4},{2,6},{4,0},{6,2},{1,5},{3,7},{5,1},{7,3},{8,12},{10,14},{12... | collective-permute-start | bytes 196616 | tf_op jit(solution)/shard_map/ppermute | solution.py:138
  63.5 6.2 %collective-permute-start.10 = (bf16[2,1,128,128]{3,2,0,1:T(8,128)(2,1)S(1)}, bf16[2,1,128,128]{3,2,0,1:T(8,128)(2,1)S(1)}, u32[]{:S(2)}, u32[]{:S(2)}) collective-permute-start(bf16[2,1,128,128]{3,2,0,1:T(8,128)(2,1)S(1)} %get-tuple-element.64), channel_id=1, source_target_pairs={{0,6},{2,4},{4,2},{6,0},{1,7},{3,5},{5,3},{7,1},{8,14},{10,12},{12... | collective-permute-start | bytes 196616 | tf_op jit(solution)/shard_map/ppermute | solution.py:138
  81.7 0.7 copy-start.4
  82.6 2.8 %collective-permute-start.11 = (bf16[2,1,64,128]{3,2,1,0:T(8,128)(2,1)S(1)}, bf16[2,1,64,128]{3,2,1,0:T(8,128)(2,1)S(1)}, u32[]{:S(2)}, u32[]{:S(2)}) collective-permute-start(bf16[2,1,64,128]{3,2,1,0:T(8,128)(2,1)S(1)} %get-tuple-element.59), channel_id=1, source_target_pairs={{0,1},{2,3},{4,5},{6,7},{8,9},{10,11},{12,13},{14,15},{16,17},{18,... | collective-permute-start | bytes 98312 | tf_op jit(solution)/shard_map/ppermute | solution.py:26
  83.9 3.1 %collective-permute-start.12 = (bf16[2,1,64,128]{3,2,1,0:T(8,128)(2,1)S(1)}, bf16[2,1,64,128]{3,2,1,0:T(8,128)(2,1)S(1)}, u32[]{:S(2)}, u32[]{:S(2)}) collective-permute-start(bf16[2,1,64,128]{3,2,1,0:T(8,128)(2,1)S(1)} %get-tuple-element.60), channel_id=1, source_target_pairs={{1,0},{3,2},{5,4},{7,6},{9,8},{11,10},{13,12},{15,14},{17,16},{19,... | collective-permute-start | bytes 98312 | tf_op jit(solution)/shard_map/ppermute | solution.py:28
  89.7 11.0 %copy-start.13 = (bf16[2,8,64,128]{3,2,1,0:T(8,128)(2,1)}, bf16[2,8,64,128]{3,2,1,0:T(8,128)(2,1)S(1)}, u32[]{:S(2)}) copy-start(bf16[2,8,64,128]{3,2,1,0:T(8,128)(2,1)S(1)} %add_convert_fusion.2) | copy-start | bytes 786436
  89.7 10.9 %collective-permute-start.13 = (bf16[2,8,64,128]{3,2,1,0:T(8,128)(2,1)S(1)}, bf16[2,8,64,128]{3,2,1,0:T(8,128)(2,1)S(1)}, u32[]{:S(2)}, u32[]{:S(2)}) collective-permute-start(bf16[2,8,64,128]{3,2,1,0:T(8,128)(2,1)S(1)} %add_convert_fusion.2), channel_id=1, source_target_pairs={{8,0},{16,8},{24,16},{9,1},{17,9},{25,17},{10,2},{18,10},{26,18},{... | collective-permute-start | bytes 786440 | tf_op jit(solution)/shard_map/ppermute | solution.py:38
  100.6 4.8 %collective-permute-start.14 = (bf16[2,1,128,128]{3,2,0,1:T(8,128)(2,1)S(1)}, bf16[2,1,128,128]{3,2,0,1:T(8,128)(2,1)S(1)}, u32[]{:S(2)}, u32[]{:S(2)}) collective-permute-start(bf16[2,1,128,128]{3,2,0,1:T(8,128)(2,1)S(1)} %get-tuple-element.56), channel_id=1, source_target_pairs={{0,2},{2,0},{4,6},{6,4},{1,3},{3,1},{5,7},{7,5},{8,10},{10,8},{12,... | collective-permute-start | bytes 196616 | tf_op jit(solution)/shard_map/ppermute | solution.py:138
  101.8 7.8 %collective-permute-start.15 = (bf16[2,1,128,128]{3,2,0,1:T(8,128)(2,1)S(1)}, bf16[2,1,128,128]{3,2,0,1:T(8,128)(2,1)S(1)}, u32[]{:S(2)}, u32[]{:S(2)}) collective-permute-start(bf16[2,1,128,128]{3,2,0,1:T(8,128)(2,1)S(1)} %get-tuple-element.55), channel_id=1, source_target_pairs={{0,4},{2,6},{4,0},{6,2},{1,5},{3,7},{5,1},{7,3},{8,12},{10,14},{12... | collective-permute-start | bytes 196616 | tf_op jit(solution)/shard_map/ppermute | solution.py:138
  102.8 6.7 %collective-permute-start.16 = (bf16[2,1,128,128]{3,2,0,1:T(8,128)(2,1)S(1)}, bf16[2,1,128,128]{3,2,0,1:T(8,128)(2,1)S(1)}, u32[]{:S(2)}, u32[]{:S(2)}) collective-permute-start(bf16[2,1,128,128]{3,2,0,1:T(8,128)(2,1)S(1)} %get-tuple-element.54), channel_id=1, source_target_pairs={{0,6},{2,4},{4,2},{6,0},{1,7},{3,5},{5,3},{7,1},{8,14},{10,12},{12... | collective-permute-start | bytes 196616 | tf_op jit(solution)/shard_map/ppermute | solution.py:138
  121.5 0.7 copy-start.6
  122.5 2.8 %collective-permute-start.17 = (bf16[2,1,64,128]{3,2,1,0:T(8,128)(2,1)S(1)}, bf16[2,1,64,128]{3,2,1,0:T(8,128)(2,1)S(1)}, u32[]{:S(2)}, u32[]{:S(2)}) collective-permute-start(bf16[2,1,64,128]{3,2,1,0:T(8,128)(2,1)S(1)} %get-tuple-element.49), channel_id=1, source_target_pairs={{0,1},{2,3},{4,5},{6,7},{8,9},{10,11},{12,13},{14,15},{16,17},{18,... | collective-permute-start | bytes 98312 | tf_op jit(solution)/shard_map/ppermute | solution.py:26
  123.8 3.1 %collective-permute-start.18 = (bf16[2,1,64,128]{3,2,1,0:T(8,128)(2,1)S(1)}, bf16[2,1,64,128]{3,2,1,0:T(8,128)(2,1)S(1)}, u32[]{:S(2)}, u32[]{:S(2)}) collective-permute-start(bf16[2,1,64,128]{3,2,1,0:T(8,128)(2,1)S(1)} %get-tuple-element.50), channel_id=1, source_target_pairs={{1,0},{3,2},{5,4},{7,6},{9,8},{11,10},{13,12},{15,14},{17,16},{19,... | collective-permute-start | bytes 98312 | tf_op jit(solution)/shard_map/ppermute | solution.py:28
  130.2 11.0 %collective-permute-start.19 = (bf16[2,8,64,128]{3,2,1,0:T(8,128)(2,1)}, bf16[2,8,64,128]{3,2,1,0:T(8,128)(2,1)}, u32[]{:S(2)}, u32[]{:S(2)}) collective-permute-start(bf16[2,8,64,128]{3,2,1,0:T(8,128)(2,1)} %add_convert_fusion.1), channel_id=1, source_target_pairs={{8,0},{16,8},{24,16},{9,1},{17,9},{25,17},{10,2},{18,10},{26,18},{... | collective-permute-start | bytes 786440 | tf_op jit(solution)/shard_map/ppermute | solution.py:38
  142.8 9.6 %collective-permute-start.20 = (bf16[2,1,128,128]{3,2,0,1:T(8,128)(2,1)}, bf16[2,1,128,128]{3,2,0,1:T(8,128)(2,1)}, u32[]{:S(2)}, u32[]{:S(2)}) collective-permute-start(bf16[2,1,128,128]{3,2,0,1:T(8,128)(2,1)} %get-tuple-element.46), channel_id=1, source_target_pairs={{0,2},{2,0},{4,6},{6,4},{1,3},{3,1},{5,7},{7,5},{8,10},{10,8},{12,... | collective-permute-start | bytes 196616 | tf_op jit(solution)/shard_map/ppermute | solution.py:138
  143.9 8.6 %collective-permute-start.21 = (bf16[2,1,128,128]{3,2,0,1:T(8,128)(2,1)}, bf16[2,1,128,128]{3,2,0,1:T(8,128)(2,1)}, u32[]{:S(2)}, u32[]{:S(2)}) collective-permute-start(bf16[2,1,128,128]{3,2,0,1:T(8,128)(2,1)} %get-tuple-element.45), channel_id=1, source_target_pairs={{0,4},{2,6},{4,0},{6,2},{1,5},{3,7},{5,1},{7,3},{8,12},{10,14},{12... | collective-permute-start | bytes 196616 | tf_op jit(solution)/shard_map/ppermute | solution.py:138
  145.0 7.4 %collective-permute-start.22 = (bf16[2,1,128,128]{3,2,0,1:T(8,128)(2,1)}, bf16[2,1,128,128]{3,2,0,1:T(8,128)(2,1)}, u32[]{:S(2)}, u32[]{:S(2)}) collective-permute-start(bf16[2,1,128,128]{3,2,0,1:T(8,128)(2,1)} %get-tuple-element.44), channel_id=1, source_target_pairs={{0,6},{2,4},{4,2},{6,0},{1,7},{3,5},{5,3},{7,1},{8,14},{10,12},{12... | collective-permute-start | bytes 196616 | tf_op jit(solution)/shard_map/ppermute | solution.py:138
  148.1 4.4 %copy-start.17 = (bf16[1,2,1,128,128]{4,3,1,2,0:T(8,128)(2,1)S(1)}, bf16[1,2,1,128,128]{4,3,1,2,0:T(8,128)(2,1)}, u32[]{:S(2)}) copy-start(bf16[1,2,1,128,128]{4,3,1,2,0:T(8,128)(2,1)} %get-tuple-element.43) | copy-start | bytes 196612
  148.1 12.4 %all-to-all-start.4 = ((bf16[2,4,128,128]{2,3,0,1:T(8,128)(2,1)}), bf16[2,4,128,128]{2,3,0,1:T(8,128)(2,1)}, u32[]{:S(2)}, u32[]{:S(2)}) async-start(bf16[2,4,128,128]{2,3,0,1:T(8,128)(2,1)} %multiply_convert_fusion), calls=%async_computation.4 | async-start | bytes 524288 | tf_op jit(solution)/shard_map/all_to_all | solution.py:124
  154.0 0.9 copy-start.9
  160.5 10.2 %all-to-all-start.3 = ((bf16[8,1,128,128]{3,2,1,0:T(8,128)(2,1)}), bf16[8,1,128,128]{3,2,1,0:T(8,128)(2,1)S(1)}, u32[]{:S(2)}, u32[]{:S(2)}) async-start(bf16[8,1,128,128]{3,2,1,0:T(8,128)(2,1)} %bitcast.571), calls=%async_computation.3 | async-start | bytes 524288 | tf_op jit(solution)/shard_map/all_to_all | solution.py:92
  163.9 73.8 %all-reduce.13.cloned.1.call-start = ((), (), s32[]{:S(2)}) async-start(), calls=%async_computation.5 | async-start | bytes 1572864 | tf_op jit(solution)/shard_map/psum | solution.py:177
  172.7 1.0 copy-start.3
  172.7 1.0 copy-start.5
  172.7 1.1 copy-start.7
  174.5 2.6 %copy-start.22 = (bf16[2,1,64,128]{3,2,1,0:T(8,128)(2,1)S(1)}, bf16[2,1,64,128]{3,2,1,0:T(8,128)(2,1)}, u32[]{:S(2)}) copy-start(bf16[2,1,64,128]{3,2,1,0:T(8,128)(2,1)} %copy-done.21) | copy-start | bytes 98308
  174.6 4.9 %collective-permute-start.23 = (bf16[2,1,64,128]{3,2,1,0:T(8,128)(2,1)S(1)}, bf16[2,1,64,128]{3,2,1,0:T(8,128)(2,1)S(1)}, u32[]{:S(2)}, u32[]{:S(2)}) collective-permute-start(bf16[2,1,64,128]{3,2,1,0:T(8,128)(2,1)S(1)} %get-tuple-element.39), channel_id=1, source_target_pairs={{0,1},{2,3},{4,5},{6,7},{8,9},{10,11},{12,13},{14,15},{16,17},{18,... | collective-permute-start | bytes 98312 | tf_op jit(solution)/shard_map/ppermute | solution.py:26
  175.9 3.6 %collective-permute-start.24 = (bf16[2,1,64,128]{3,2,1,0:T(8,128)(2,1)S(1)}, bf16[2,1,64,128]{3,2,1,0:T(8,128)(2,1)S(1)}, u32[]{:S(2)}, u32[]{:S(2)}) collective-permute-start(bf16[2,1,64,128]{3,2,1,0:T(8,128)(2,1)S(1)} %get-tuple-element.40), channel_id=1, source_target_pairs={{1,0},{3,2},{5,4},{7,6},{9,8},{11,10},{13,12},{15,14},{17,16},{19,... | collective-permute-start | bytes 98312 | tf_op jit(solution)/shard_map/ppermute | solution.py:28
  177.5 0.8 copy-start.20
  181.7 1.0 copy-start.12
  181.7 1.0 copy-start.14
  237.6 2.0 copy-start.18
Sparse Core Ops, SparseCore 0:
  179.5 58.0 all-reduce.12
